TPU v7x, 128 devices: a whole 4x4x4 slice. The times are simulated.
128 devices in a mesh: pipe: 4 (over x_hi, core), dp: 32 (over y, z, x_lo).
Axes of the slice: x: 4 (x_hi: 2, x_lo: 2; x = x_hi * 2 + x_lo), y: 4, z: 4, core: 2. Of those that a mesh axis runs over, the one named last changes fastest.
Arguments:
- layer_input: bfloat16 [4, 4096, 8192], P('pipe', 'dp'), may hold values from -130 to 130
- queries: bfloat16 [4, 4096, 4096], P('pipe', 'dp'), may hold values from -35 to 35
- out_grad: bfloat16 [4, 4096, 4096], P('pipe', 'dp'), may hold values from -6 to 6
- top_grad: bfloat16 [4096, 8192], P('dp'), may hold values from -4 to 4
- norm_gain: bfloat16 [4, 8192], P('pipe', 'dp'), may hold values from 0.5 to 1.5
- key_weight: bfloat16 [4, 8192, 512], P('pipe', 'dp'), may hold values from -0.0625 to 0.0625
- value_weight: bfloat16 [4, 8192, 512], P('pipe', 'dp'), may hold values from -0.0625 to 0.0625
- weight_exponents: int32 [4, 2, 64, 4], P('pipe', None, 'dp'), may hold values from -1 to 1
- doc_lengths: int32 [64], replicated, may hold values from 1 to 512, 4096 in all
Outputs:
- input_grad: bfloat16 [4, 4096, 8192], P('pipe', 'dp')
- query_grad: bfloat16 [4, 4096, 4096], P('pipe', 'dp')
- key_weight_grad: float32 [4, 8192, 512], P('pipe', 'dp')
- value_weight_grad: float32 [4, 8192, 512], P('pipe', 'dp')
- gain_grad: float32 [4, 8192], P('pipe', 'dp')
Inputs may be any that keep to these rules, and one draw needn't show every extreme that they name: `doc_lengths`: the lengths sum to 4096; the longest is exactly 512. `weight_exponents`: one exponent of two for each 128 x 128 block.
All inputs are finite; a program needn't handle non-finite values.
Results may differ from a plain program's by a relative error of at most 0.035.
The roundings to bfloat16 on the way count: a program that leaves them out, or rounds other values in their place, can miss the bound.
Values may be sent and summed in bfloat16 or wider, within the bound.
A program may use at most 192 MiB of HBM per device.

v0:
```python
from functools import reduce
import math
import jax
import jax.numpy as jnp
from jax import lax
from jax.sharding import PartitionSpec as P

KV_HEADS = 4
Q_PER_KV = 8
HEAD = 128
BLOCK = 128
REACH = 4
theta_base = 500000.0
eps_norm = 1e-05
masked_score = -1e30


def passed_along(block, axis, distance):
    devices = range(lax.axis_size(axis))
    route = [(i - distance, i) for i in devices if i - distance in devices]
    return lax.ppermute(block, axis, route)


def rotary_tables(positions, head_size):
    half_size = head_size // 2
    frequency = theta_base ** (-(jnp.arange(half_size).astype(jnp.float32) * 2.0 / head_size))
    angles = positions.astype(jnp.float32)[:, None] * frequency[None, :]
    return (jnp.cos(angles)[:, None, :], jnp.sin(angles)[:, None, :])


def rotate(values, cosine, sine):
    half_size = values.shape[-1] // 2
    first = values[..., :half_size]
    second = values[..., half_size:]
    return jnp.concatenate(
        [first * cosine - second * sine, second * cosine + first * sine], axis=-1
    )


def unrotate(grads, cosine, sine):
    half_size = grads.shape[-1] // 2
    first = grads[..., :half_size]
    second = grads[..., half_size:]
    return jnp.concatenate(
        [first * cosine + second * sine, second * cosine - first * sine], axis=-1
    )


def doc_info(token_index, doc_lengths):
    starts = jnp.cumsum(doc_lengths) - doc_lengths
    before = starts[None, :] <= token_index[:, None]
    doc_number = jnp.sum(before.astype(jnp.int32), axis=1) - 1
    doc_start = jnp.max(jnp.where(before, starts[None, :], 0), axis=1)
    return (doc_number, token_index - doc_start)


def dequantize(values, exponents, block_side):
    row_blocks, col_blocks = exponents.shape
    factors = jnp.exp2(exponents.astype(jnp.float32))
    shaped = values.astype(jnp.float32).reshape(row_blocks, block_side, col_blocks, block_side)
    return (shaped * factors[:, None, :, None]).reshape(values.shape).astype(jnp.bfloat16)


def guarded(compute):
    result = compute()
    return result


def on_device(
    layer_input,
    queries,
    out_grad,
    top_grad,
    norm_gain,
    key_weight,
    value_weight,
    weight_exponents,
    doc_lengths,
):
    local_rows = layer_input.shape[1]
    kv_heads = KV_HEADS
    group_size = Q_PER_KV
    head_size = HEAD
    dp_index = lax.axis_index("dp")
    section_index = lax.axis_index("pipe")
    sections = lax.axis_size("pipe")
    key_local = dequantize(key_weight[0], weight_exponents[0, 0], BLOCK)
    value_local = dequantize(value_weight[0], weight_exponents[0, 1], BLOCK)
    key_full, value_full, gain_full = (
        lax.all_gather(key_local, "dp", axis=0, tiled=True),
        lax.all_gather(value_local, "dp", axis=0, tiled=True),
        lax.all_gather(norm_gain[0], "dp", axis=0, tiled=True),
    )
    inputs = layer_input[0].astype(jnp.float32)
    root_mean = jnp.sqrt(jnp.mean(inputs * inputs, axis=1, keepdims=True) + eps_norm)
    normed = inputs / root_mean
    gain_f = gain_full.astype(jnp.float32)
    hidden = (normed * gain_f).astype(jnp.bfloat16)
    token_index = dp_index * local_rows + jnp.arange(local_rows)
    query_doc, query_pos = doc_info(token_index, doc_lengths)
    cosine, sine = rotary_tables(query_pos, head_size)
    key_proj = jnp.dot(hidden, key_full, preferred_element_type=jnp.float32).reshape(
        local_rows, kv_heads, head_size
    )
    keys_own = rotate(key_proj, cosine, sine).astype(jnp.bfloat16)
    values_own = (
        jnp.dot(hidden, value_full, preferred_element_type=jnp.float32)
        .astype(jnp.bfloat16)
        .reshape(local_rows, kv_heads, head_size)
    )
    key_blocks = [None] * (REACH + 1)
    value_blocks = [None] * (REACH + 1)
    key_blocks[REACH] = keys_own
    value_blocks[REACH] = values_own
    own_pair = jnp.stack((keys_own, values_own))
    for distance in range(1, REACH + 1):
        got_pair = passed_along(own_pair, "dp", distance)
        key_blocks[REACH - distance] = got_pair[0]
        value_blocks[REACH - distance] = got_pair[1]
    inv_root = 1.0 / math.sqrt(head_size)
    query_groups = queries[0].reshape(local_rows, kv_heads, group_size, head_size)
    grad_groups = out_grad[0].reshape(local_rows, kv_heads, group_size, head_size)
    visibility = []
    seen_flags = []
    for block_number in range(REACH + 1):
        key_index = (dp_index - REACH + block_number) * local_rows + jnp.arange(local_rows)
        key_doc, unused = doc_info(key_index, doc_lengths)
        visible = (
            (key_index[None, :] >= 0)
            & (key_doc[None, :] == query_doc[:, None])
            & (key_index[None, :] <= token_index[:, None])
        )
        visibility.append(visible)
        seen_flags.append(jnp.any(visible))

    def score_block(block_number):

        def compute():
            raw_scores = jnp.einsum(
                "qkgd,tkd->kgqt",
                query_groups,
                key_blocks[block_number],
                preferred_element_type=jnp.float32,
            )
            return jnp.where(
                visibility[block_number][None, None], raw_scores * inv_root, masked_score
            )

        return guarded(compute)

    scores = [score_block(block_number) for block_number in range(REACH + 1)]
    row_max = reduce(jnp.maximum, [jnp.max(member, axis=3, keepdims=True) for member in scores])
    exp_scores = [jnp.exp(member - row_max) for member in scores]
    row_total = reduce(jnp.add, [jnp.sum(member, axis=3, keepdims=True) for member in exp_scores])
    softmax_out = [member / row_total for member in exp_scores]
    probs_low = [member.astype(jnp.bfloat16) for member in softmax_out]

    def attend_block(block_number):

        def compute():
            return jnp.einsum(
                "kgqt,tkd->qkgd",
                probs_low[block_number],
                value_blocks[block_number],
                preferred_element_type=jnp.float32,
            )

        return guarded(compute)

    attended = reduce(jnp.add, [attend_block(block_number) for block_number in range(REACH + 1)])
    out_dot = jnp.transpose(jnp.sum(grad_groups.astype(jnp.float32) * attended, axis=3), (1, 2, 0))[
        ..., None
    ]

    def grads_block(block_number):

        def compute():
            value_term = jnp.einsum(
                "kgqt,qkgd->tkd",
                probs_low[block_number],
                grad_groups,
                preferred_element_type=jnp.float32,
            )
            prob_grad = jnp.einsum(
                "qkgd,tkd->kgqt",
                grad_groups,
                value_blocks[block_number],
                preferred_element_type=jnp.float32,
            )
            score_grads = (softmax_out[block_number] * (prob_grad - out_dot)).astype(jnp.bfloat16)
            query_term = jnp.einsum(
                "kgqt,tkd->qkgd",
                score_grads,
                key_blocks[block_number],
                preferred_element_type=jnp.float32,
            )
            key_term = (
                jnp.einsum(
                    "kgqt,qkgd->tkd", score_grads, query_groups, preferred_element_type=jnp.float32
                )
                * inv_root
            )
            return (query_term, key_term.astype(jnp.bfloat16), value_term.astype(jnp.bfloat16))

        return guarded(compute)

    block_grads = [grads_block(block_number) for block_number in range(REACH + 1)]
    query_grad = (
        (reduce(jnp.add, [member[0] for member in block_grads]) * inv_root)
        .astype(jnp.bfloat16)
        .reshape(1, local_rows, -1)
    )
    key_sum = block_grads[REACH][1].astype(jnp.float32)
    value_sum = block_grads[REACH][2].astype(jnp.float32)
    for distance in range(1, REACH + 1):
        sent_pair = jnp.stack((block_grads[REACH - distance][1], block_grads[REACH - distance][2]))
        back_pair = passed_along(sent_pair, "dp", -distance)
        key_sum = key_sum + back_pair[0].astype(jnp.float32)
        value_sum = value_sum + back_pair[1].astype(jnp.float32)
    key_grads = unrotate(key_sum, cosine, sine).astype(jnp.bfloat16).reshape(local_rows, -1)
    value_grads = value_sum.astype(jnp.bfloat16).reshape(local_rows, -1)
    hidden_grad = jnp.einsum(
        "tc,dc->td", key_grads, key_full, preferred_element_type=jnp.float32
    ) + jnp.einsum("tc,dc->td", value_grads, value_full, preferred_element_type=jnp.float32)
    gain_term = jnp.sum(hidden_grad * normed, axis=0)
    scaled_grad = hidden_grad * gain_f
    branch = (
        scaled_grad - normed * jnp.mean(scaled_grad * normed, axis=1, keepdims=True)
    ) / root_mean
    last_section = sections - 1
    carried = jnp.where(
        section_index == last_section,
        (top_grad.astype(jnp.float32) + branch).astype(jnp.bfloat16),
        jnp.zeros_like(top_grad),
    )
    for step_number in range(sections - 1):
        received = passed_along(carried, "pipe", -1)
        carried = jnp.where(
            section_index == last_section - 1 - step_number,
            (received.astype(jnp.float32) + branch).astype(jnp.bfloat16),
            carried,
        )
    key_full_grad = jnp.einsum("tr,tc->rc", hidden, key_grads, preferred_element_type=jnp.float32)
    value_full_grad = jnp.einsum(
        "tr,tc->rc", hidden, value_grads, preferred_element_type=jnp.float32
    )
    key_wgrad, value_wgrad, gain_grad = (
        lax.psum_scatter(
            key_full_grad.astype(jnp.bfloat16), "dp", scatter_dimension=0, tiled=True
        ).astype(jnp.float32),
        lax.psum_scatter(
            value_full_grad.astype(jnp.bfloat16), "dp", scatter_dimension=0, tiled=True
        ).astype(jnp.float32),
        lax.psum_scatter(
            gain_term.astype(jnp.bfloat16), "dp", scatter_dimension=0, tiled=True
        ).astype(jnp.float32),
    )
    return (carried[None], query_grad, key_wgrad[None], value_wgrad[None], gain_grad[None])


def solution(mesh):
    in_specs = (
        P("pipe", "dp", None),
        P("pipe", "dp", None),
        P("pipe", "dp", None),
        P("dp", None),
        P("pipe", "dp"),
        P("pipe", "dp", None),
        P("pipe", "dp", None),
        P("pipe", None, "dp", None),
        P(),
    )
    out_specs = (
        P("pipe", "dp", None),
        P("pipe", "dp", None),
        P("pipe", "dp", None),
        P("pipe", "dp", None),
        P("pipe", "dp"),
    )
    return jax.shard_map(
        on_device, mesh=mesh, in_specs=in_specs, out_specs=out_specs, check_vma=False
    )
```

profile of v0, /device:TPU:0, one launch (start us, length us, event | category | flops | bytes accessed | tf_op | source)
XLA Modules:
  0.0 965.6 jit_solution(9609781831915114517)
XLA Ops:
  7.3 0.8 exponential_bitcast_fusion.1
  8.2 1.7 fusion.70
  10.2 0.8 fusion.71
  11.0 82.9 %all-gather = bf16[1,8192]{1,0:T(2,128)(2,1)S(1)} all-gather(bf16[1,256]{1,0:T(2,128)(2,1)S(1)} %copy-done.38), channel_id=2, replica_groups=mesh['pipe'=4,'dp'=32] {'dp'}, dimensions={1}, use_global_device_ids=true | all-gather | bytes 16896 | tf_op jit(solution)/shard_map/all_gather | solution.py:92
  94.6 0.7 copy.192
  95.5 2.1 fusion.2
  97.9 0.9 compare_and_fusion.3
  98.8 104.8 %all-gather.6.cloned.1.call-done = bf16[8192,512]{1,0:T(8,128)(2,1)} async-done(((bf16[256,512]{1,0:T(8,128)(2,1)}), bf16[8192,512]{1,0:T(8,128)(2,1)}) %all-gather.6.cloned.1.call-update) | async-done | bytes 8388624 | tf_op jit(solution)/shard_map/all_gather | solution.py:91
  203.7 5.3 fusion.49
  209.2 184.8 %all-gather.4.cloned.1.call-done = bf16[8192,512]{1,0:T(8,128)(2,1)} async-done(((bf16[256,512]{1,0:T(8,128)(2,1)}), bf16[8192,512]{1,0:T(8,128)(2,1)}) %all-gather.4.cloned.1.call-update) | async-done | bytes 8388624 | tf_op jit(solution)/shard_map/all_gather | solution.py:90
  393.9 12.0 %copy.180 = bf16[512,8192]{1,0:T(8,128)(2,1)} copy(bf16[512,8192]{0,1:T(8,128)(2,1)} %bitcast.450) | data formatting | bytes 16777216 | tf_op jit(solution)/shard_map/dot_general | solution.py:102
  406.0 6.4 fusion.22
  412.5 0.7 pad_maximum_fusion
  413.2 1.3 collective-permute-start.3
  414.5 1.5 collective-permute-start.2
  416.0 4.1 collective-permute-start.1
  420.1 5.4 collective-permute-start
  425.6 1.4 fusion.100
  427.1 9.1 collective-permute-done
  436.2 0.7 fusion.103
  436.9 0.7 fusion.104
  437.6 0.7 fusion.102
  438.3 0.7 fusion.101
  439.0 3.3 fusion.32
  442.3 2.4 fusion.65
  448.2 1.0 fusion.19
  449.2 0.7 fusion.12
  450.9 0.7 fusion.14
  452.2 0.7 fusion.16
  454.1 0.7 fusion.18
  455.5 1.4 collective-permute-start.4
  456.9 1.3 collective-permute-start.5
  458.3 1.3 collective-permute-start.6
  459.6 1.5 collective-permute-start.7
  461.1 4.6 collective-permute-done.4
  465.7 7.0 collective-permute-done.5
  472.7 1.1 collective-permute-done.7
  474.5 0.6 copy-done.52
  475.1 5.7 convolution_convert_fusion
  481.0 2.4 fusion.21
  483.5 0.7 convert_add_fusion.4
  484.5 1.0 copy-done.2
  485.5 5.7 convolution_convert_fusion.1
  491.2 6.4 fusion.106
  497.6 6.0 multiply_reduce_fusion
  503.7 2.8 fusion.6
  506.5 1.3 collective-permute-start.8
  507.8 4.9 collective-permute-done.8
  512.7 4.9 fusion.7
  517.6 1.5 collective-permute-start.9
  519.1 71.2 %collective-permute-done.9 = bf16[128,8192]{1,0:T(8,128)(2,1)} collective-permute-done((bf16[128,8192]{1,0:T(8,128)(2,1)}, bf16[128,8192]{1,0:T(8,128)(2,1)}, u32[]{:S(2)}, u32[]{:S(2)}) %collective-permute-start.9) | collective-permute-done | bytes 2097184 | tf_op jit(solution)/shard_map/ppermute | solution.py:21
  590.3 6.0 fusion.8
  596.3 1.3 collective-permute-start.10
  597.6 1.2 dynamic-slice
  599.5 1.7 fusion.81
  601.7 0.8 copy-done.6
  603.9 0.8 copy-done.13
  604.7 0.7 multiply_convert_fusion.2
  605.5 1.3 copy.233
  606.8 171.8 %all-reduce = bf16[8192]{0:T(1024)(128)(2,1)S(1)} all-reduce(bf16[8192]{0:T(1024)(128)(2,1)S(1)} %get-tuple-element.25), channel_id=5, replica_groups=mesh['pipe'=4,'dp'=32] {'dp'}, use_global_device_ids=true, to_apply=%region_23.24.clone | all-reduce | flops 8192 | bytes 32768
  779.3 7.0 fusion.10
  786.3 1.8 bitcast_convert_fusion
  788.1 168.9 %reduce-scatter.3.cloned.1.call-done = bf16[256,512]{1,0:T(8,128)(2,1)} async-done(((bf16[8192,512]{1,0:T(8,128)(2,1)}), bf16[256,512]{1,0:T(8,128)(2,1)}) %reduce-scatter.3.cloned.1.call-update) | async-done | bytes 262160 | tf_op jit(solution)/shard_map/reduce_scatter | solution.py:248
  957.0 1.8 bitcast_convert_fusion.1
  (171 shorter events, 12.3 us)
Async XLA Ops:
  7.2 3.0 copy-start.28
  7.2 3.9 copy-start.38
  7.2 86.8 %copy-start.43 = (s32[64]{0:T(128)S(1)}, s32[64]{0:T(128)}, u32[]{:S(2)}) copy-start(s32[64]{0:T(128)} %param.17) | copy-start | bytes 772
  7.2 87.1 %copy-start.10 = (bf16[1,128,4096]{2,1,0:T(8,128)(2,1)S(1)}, bf16[1,128,4096]{2,1,0:T(8,128)(2,1)}, u32[]{:S(2)}) copy-start(bf16[1,128,4096]{2,1,0:T(8,128)(2,1)} %param.10) | copy-start | bytes 3145732
  7.2 196.4 %all-gather.6.cloned.1.call-start = ((), (), s32[]{:S(2)}) async-start(), calls=%async_computation.3 | async-start | bytes 8650752 | tf_op jit(solution)/shard_map/all_gather | solution.py:91
  9.9 384.0 %all-gather.4.cloned.1.call-start = ((), (), s32[]{:S(2)}) async-start(), calls=%async_computation.2 | async-start | bytes 8650752 | tf_op jit(solution)/shard_map/all_gather | solution.py:90
  10.0 84.6 %copy-start.11 = (bf16[1,128,4096]{2,1,0:T(8,128)(2,1)S(1)}, bf16[1,128,4096]{2,1,0:T(8,128)(2,1)}, u32[]{:S(2)}) copy-start(bf16[1,128,4096]{2,1,0:T(8,128)(2,1)} %param.11) | copy-start | bytes 3145732
  11.0 775.3 %reduce-scatter.5.cloned.1.call-start = ((), (), s32[]{:S(2)}) async-start(), calls=%async_computation.5 | async-start | bytes 8650752 | tf_op jit(solution)/shard_map/reduce_scatter | solution.py:251
  94.0 312.0 %copy-start.29 = (f32[1,8192]{1,0:T(1,128)}, f32[1,8192]{1,0:T(1,128)S(1)}, u32[]{:S(2)}) copy-start(f32[1,8192]{1,0:T(1,128)S(1)} %convert_element_type.409) | copy-start | bytes 98308
  97.6 308.4 %copy-start.39 = (f32[128]{0:T(128)}, f32[128]{0:T(128)S(1)}, u32[]{:S(2)}) copy-start(f32[128]{0:T(128)S(1)} %add_sqrt_fusion) | copy-start | bytes 1540
  97.9 314.5 %copy-start.24 = (f32[128,64]{0,1:T(8,128)}, f32[128,64]{0,1:T(8,128)S(1)}, u32[]{:S(2)}) copy-start(f32[128,64]{0,1:T(8,128)S(1)} %get-tuple-element.56) | copy-start | bytes 98308
  97.9 314.5 %copy-start.26 = (f32[128,64]{0,1:T(8,128)}, f32[128,64]{0,1:T(8,128)S(1)}, u32[]{:S(2)}) copy-start(f32[128,64]{0,1:T(8,128)S(1)} %get-tuple-element.57) | copy-start | bytes 98308
  413.2 25.1 %collective-permute-start.3 = (bf16[2,128,4,128]{1,3,2,0:T(8,128)(2,1)}, bf16[2,128,4,128]{1,3,2,0:T(8,128)(2,1)S(1)}, u32[]{:S(2)}, u32[]{:S(2)}) collective-permute-start(bf16[2,128,4,128]{1,3,2,0:T(8,128)(2,1)} %pad_maximum_fusion), channel_id=1, source_target_pairs={{0,1},{1,2},{2,3},{3,4},{4,5},{5,6},{6,7},{7,8},{8,9},{9,10},{10,1... | collective-permute-start | bytes 786440 | tf_op jit(solution)/shard_map/ppermute | solution.py:21
  414.5 23.1 %collective-permute-start.2 = (bf16[2,128,4,128]{1,3,2,0:T(8,128)(2,1)}, bf16[2,128,4,128]{1,3,2,0:T(8,128)(2,1)S(1)}, u32[]{:S(2)}, u32[]{:S(2)}) collective-permute-start(bf16[2,128,4,128]{1,3,2,0:T(8,128)(2,1)} %pad_maximum_fusion), channel_id=1, source_target_pairs={{0,2},{1,3},{2,4},{3,5},{4,6},{5,7},{6,8},{7,9},{8,10},{9,11},{10,... | collective-permute-start | bytes 786440 | tf_op jit(solution)/shard_map/ppermute | solution.py:21
  416.0 20.9 %collective-permute-start.1 = (bf16[2,128,4,128]{1,3,2,0:T(8,128)(2,1)}, bf16[2,128,4,128]{1,3,2,0:T(8,128)(2,1)S(1)}, u32[]{:S(2)}, u32[]{:S(2)}) collective-permute-start(bf16[2,128,4,128]{1,3,2,0:T(8,128)(2,1)} %pad_maximum_fusion), channel_id=1, source_target_pairs={{0,3},{1,4},{2,5},{3,6},{4,7},{5,8},{6,9},{7,10},{8,11},{9,12},{10... | collective-permute-start | bytes 786440 | tf_op jit(solution)/shard_map/ppermute | solution.py:21
  420.1 16.1 %collective-permute-start = (bf16[2,128,4,128]{1,3,2,0:T(8,128)(2,1)}, bf16[2,128,4,128]{1,3,2,0:T(8,128)(2,1)S(1)}, u32[]{:S(2)}, u32[]{:S(2)}) collective-permute-start(bf16[2,128,4,128]{1,3,2,0:T(8,128)(2,1)} %pad_maximum_fusion), channel_id=1, source_target_pairs={{0,4},{1,5},{2,6},{3,7},{4,8},{5,9},{6,10},{7,11},{8,12},{9,13},{1... | collective-permute-start | bytes 786440 | tf_op jit(solution)/shard_map/ppermute | solution.py:21
  425.6 20.9 %copy-start.23 = (bf16[128,4,128,1]{0,2,3,1:T(8,128)(2,1)}, bf16[128,4,128,1]{0,2,3,1:T(8,128)(2,1)S(1)}, u32[]{:S(2)}) copy-start(bf16[128,4,128,1]{0,2,3,1:T(8,128)(2,1)S(1)} %copy.249) | copy-start | bytes 393220
  425.6 10.6 %copy-start.35 = (pred[128,128]{0,1:T(8,128)(4,1)S(1)}, pred[128,128]{0,1:T(8,128)(4,1)}, u32[]{:S(2)}) copy-start(pred[128,128]{0,1:T(8,128)(4,1)} %get-tuple-element.51) | copy-start | bytes 49156
  427.1 15.2 %copy-start = (f32[4,8,128,128]{2,3,1,0:T(8,128)}, f32[4,8,128,128]{2,3,1,0:T(8,128)S(1)}, u32[]{:S(2)}) copy-start(f32[4,8,128,128]{2,3,1,0:T(8,128)S(1)} %get-tuple-element.59) | copy-start | bytes 6291460
  427.1 9.8 %copy-start.34 = (pred[128,128]{0,1:T(8,128)(4,1)S(1)}, pred[128,128]{0,1:T(8,128)(4,1)}, u32[]{:S(2)}) copy-start(pred[128,128]{0,1:T(8,128)(4,1)} %get-tuple-element.55) | copy-start | bytes 49156
  436.2 11.6 %copy-start.17 = (bf16[2,128,4,128]{1,3,2,0:T(8,128)(2,1)}, bf16[2,128,4,128]{1,3,2,0:T(8,128)(2,1)S(1)}, u32[]{:S(2)}) copy-start(bf16[2,128,4,128]{1,3,2,0:T(8,128)(2,1)S(1)} %collective-permute-done) | copy-start | bytes 786436
  436.9 10.5 %copy-start.14 = (bf16[2,128,4,128]{1,3,2,0:T(8,128)(2,1)}, bf16[2,128,4,128]{1,3,2,0:T(8,128)(2,1)S(1)}, u32[]{:S(2)}) copy-start(bf16[2,128,4,128]{1,3,2,0:T(8,128)(2,1)S(1)} %collective-permute-done.1) | copy-start | bytes 786436
  438.3 9.9 %copy-start.20 = (bf16[2,128,4,128]{1,3,2,0:T(8,128)(2,1)}, bf16[2,128,4,128]{1,3,2,0:T(8,128)(2,1)S(1)}, u32[]{:S(2)}) copy-start(bf16[2,128,4,128]{1,3,2,0:T(8,128)(2,1)S(1)} %collective-permute-done.3) | copy-start | bytes 786436
  442.3 11.3 %copy-start.36 = (f32[4,8,128]{2,1,0:T(8,128)}, f32[4,8,128]{2,1,0:T(8,128)S(1)}, u32[]{:S(2)}) copy-start(f32[4,8,128]{2,1,0:T(8,128)S(1)} %add_add_fusion) | copy-start | bytes 49156
  448.2 1.0 copy-start.18
  449.2 4.4 copy-start.37
  451.5 1.3 copy-start.5
  452.9 1.8 copy-start.7
  452.9 1.1 copy-start.21
  454.7 4.9 copy-start.12
  455.4 19.7 %copy-start.1 = (bf16[1,128,8192]{2,1,0:T(8,128)(2,1)S(1)}, bf16[1,128,8192]{2,1,0:T(8,128)(2,1)}, u32[]{:S(2)}) copy-start(bf16[1,128,8192]{2,1,0:T(8,128)(2,1)} %param.9) | copy-start | bytes 6291460
  455.5 19.7 %copy-start.30 = (f32[1,8192]{1,0:T(1,128)S(1)}, f32[1,8192]{1,0:T(1,128)}, u32[]{:S(2)}) copy-start(f32[1,8192]{1,0:T(1,128)} %copy-done.29) | copy-start | bytes 98308
  455.5 19.7 %copy-start.40 = (f32[128]{0:T(128)S(1)}, f32[128]{0:T(128)}, u32[]{:S(2)}) copy-start(f32[128]{0:T(128)} %copy-done.39) | copy-start | bytes 1540
  455.5 10.2 %collective-permute-start.4 = (bf16[2,128,4,128]{1,3,2,0:T(8,128)(2,1)S(1)}, bf16[2,128,4,128]{1,3,2,0:T(8,128)(2,1)S(1)}, u32[]{:S(2)}, u32[]{:S(2)}) collective-permute-start(bf16[2,128,4,128]{1,3,2,0:T(8,128)(2,1)S(1)} %pad_maximum_fusion.1), channel_id=1, source_target_pairs={{1,0},{2,1},{3,2},{4,3},{5,4},{6,5},{7,6},{8,7},{9,8},{10,9},{11,1... | collective-permute-start | bytes 786440 | tf_op jit(solution)/shard_map/ppermute | solution.py:21
  456.9 15.7 %collective-permute-start.5 = (bf16[2,128,4,128]{1,3,2,0:T(8,128)(2,1)S(1)}, bf16[2,128,4,128]{1,3,2,0:T(8,128)(2,1)S(1)}, u32[]{:S(2)}, u32[]{:S(2)}) collective-permute-start(bf16[2,128,4,128]{1,3,2,0:T(8,128)(2,1)S(1)} %pad_maximum_fusion.2), channel_id=1, source_target_pairs={{2,0},{3,1},{4,2},{5,3},{6,4},{7,5},{8,6},{9,7},{10,8},{11,9},{12,... | collective-permute-start | bytes 786440 | tf_op jit(solution)/shard_map/ppermute | solution.py:21
  458.3 14.4 %collective-permute-start.6 = (bf16[2,128,4,128]{1,3,2,0:T(8,128)(2,1)S(1)}, bf16[2,128,4,128]{1,3,2,0:T(8,128)(2,1)S(1)}, u32[]{:S(2)}, u32[]{:S(2)}) collective-permute-start(bf16[2,128,4,128]{1,3,2,0:T(8,128)(2,1)S(1)} %pad_maximum_fusion.3), channel_id=1, source_target_pairs={{3,0},{4,1},{5,2},{6,3},{7,4},{8,5},{9,6},{10,7},{11,8},{12,9},{13... | collective-permute-start | bytes 786440 | tf_op jit(solution)/shard_map/ppermute | solution.py:21
  459.6 14.1 %collective-permute-start.7 = (bf16[2,128,4,128]{1,3,2,0:T(8,128)(2,1)S(1)}, bf16[2,128,4,128]{1,3,2,0:T(8,128)(2,1)S(1)}, u32[]{:S(2)}, u32[]{:S(2)}) collective-permute-start(bf16[2,128,4,128]{1,3,2,0:T(8,128)(2,1)S(1)} %pad_maximum_fusion.4), channel_id=1, source_target_pairs={{4,0},{5,1},{6,2},{7,3},{8,4},{9,5},{10,6},{11,7},{12,8},{13,9},{1... | collective-permute-start | bytes 786440 | tf_op jit(solution)/shard_map/ppermute | solution.py:21
  465.7 8.5 copy-start.44
  472.7 1.6 copy-start.46
  472.7 1.6 copy-start.48
  480.9 476.2 %reduce-scatter.3.cloned.1.call-start = ((), (), s32[]{:S(2)}) async-start(), calls=%async_computation.4 | async-start | bytes 8650752 | tf_op jit(solution)/shard_map/reduce_scatter | solution.py:248
  480.9 2.5 copy-start.45
  480.9 2.5 copy-start.47
  480.9 2.5 copy-start.49
  481.0 2.5 copy-start.51
  483.4 1.0 copy-start.9
  483.5 1.0 copy-start.25
  483.5 1.0 copy-start.27
  483.5 2.0 copy-start.2
  483.5 2.0 copy-start.31
  483.5 2.0 copy-start.41
  491.2 6.4 copy-start.3
  491.2 6.4 copy-start.53
  497.6 6.1 copy-start.4
  497.6 6.1 copy-start.32
  497.6 6.1 copy-start.42
  506.5 6.2 collective-permute-start.8
  517.6 72.7 %collective-permute-start.9 = (bf16[128,8192]{1,0:T(8,128)(2,1)}, bf16[128,8192]{1,0:T(8,128)(2,1)}, u32[]{:S(2)}, u32[]{:S(2)}) collective-permute-start(bf16[128,8192]{1,0:T(8,128)(2,1)} %fusion.7), channel_id=1, source_target_pairs={{32,0},{64,32},{96,64},{33,1},{65,33},{97,65},{34,2},{66,34},{98,6... | collective-permute-start | bytes 6291464 | tf_op jit(solution)/shard_map/ppermute | solution.py:21
  596.3 183.0 %collective-permute-start.10 = (bf16[128,8192]{1,0:T(8,128)(2,1)}, bf16[128,8192]{1,0:T(8,128)(2,1)}, u32[]{:S(2)}, u32[]{:S(2)}) collective-permute-start(bf16[128,8192]{1,0:T(8,128)(2,1)} %fusion.8), channel_id=1, source_target_pairs={{32,0},{64,32},{96,64},{33,1},{65,33},{97,65},{34,2},{66,34},{98,6... | collective-permute-start | bytes 6291464 | tf_op jit(solution)/shard_map/ppermute | solution.py:21
  599.5 1.7 copy-start.8
  601.2 1.2 copy-start.6
  601.2 1.3 copy-start.16
  603.4 1.2 copy-start.13
  603.4 1.3 copy-start.22
  (5 other events, 4.0 us)
Sparse Core Ops, SparseCore 0:
  10.3 193.3 all-gather.5
  205.9 187.9 all-gather.3
  481.0 214.5 reduce-scatter.4
  697.9 259.1 reduce-scatter.2
where the time goes:
time: 972 us; the launch traced here: 966 us
  waiting for transfers between devices  556 us (57%)
  blocking collectives  255 us (26%)
  matrix products  56.6 us (6%)
  other arithmetic  38.6 us (4%)
  starting transfers between devices  21.9 us (2%)
  local copies, waits for them, and re-layouts  21.4 us (2%)
  between operations  15.9 us (2%)
    all_gather x1, waiting for transfers between devices, on_device(): lax.all_gather(key_local, 'dp', axis=0, tiled=True)  185 us
    unnamed x1, blocking collectives  172 us
    reduce_scatter x1, waiting for transfers between devices, on_device(): lax.psum_scatter(key_full_grad.astype(jnp.bfloat16), 'dp', scatter_dimens...  169 us
    all_gather x1, waiting for transfers between devices, on_device(): lax.all_gather(value_local, 'dp', axis=0, tiled=True)  105 us
    ppermute x11, waiting for transfers between devices, passed_along(): return lax.ppermute(block, axis, route)  97.8 us
    all_gather x1, blocking collectives, on_device(): lax.all_gather(norm_gain[0], 'dp', axis=0, tiled=True)  82.9 us
    ppermute x11, starting transfers between devices, passed_along(): return lax.ppermute(block, axis, route)  21.8 us
  transfers between devices with their start and end apart: 15, of which 9 were waited for; matrix products, arithmetic and copies ran while one was open for 7% of the time, Pallas kernels for 0%

commit v1 on v0

--- a/solution.py
+++ b/solution.py
@@ -88,7 +88,15 @@
     value_local = dequantize(value_weight[0], weight_exponents[0, 1], BLOCK)
     key_full, value_full, gain_full = (
         lax.all_gather(key_local, "dp", axis=0, tiled=True),
-        lax.all_gather(value_local, "dp", axis=0, tiled=True),
+        jnp.concatenate(
+            lax.all_to_all(
+                jnp.stack([value_local] * lax.axis_size("dp")),
+                axis_name="dp",
+                split_axis=0,
+                concat_axis=0,
+            ),
+            axis=0,
+        ),
         lax.all_gather(norm_gain[0], "dp", axis=0, tiled=True),
     )
     inputs = layer_input[0].astype(jnp.float32)

time: 972 us -> 899 us (0.925)
  waiting for transfers between devices: 556 us -> 274 us
  blocking collectives: 255 us -> 454 us
  starting transfers between devices: 21.9 us -> 31.8 us
    all_gather x1, blocking collectives: 82.9 us -> 282 us  [on_device(): lax.all_gather(norm_gain[0], 'dp', axis=0, tiled=True)]
    all_gather x1, waiting for transfers between devices: 185 us -> 9.38 us  [on_device(): lax.all_gather(key_local, 'dp', axis=0, tiled=True)]
    all_gather x1 -> x0, waiting for transfers between devices: 105 us -> none  [on_device(): lax.all_gather(value_local, 'dp', axis=0, tiled=True)]
  transfers between devices with their start and end apart: 15 -> 15, of which waited for: 9 -> 7; matrix products, arithmetic and copies ran while one was open for 7% -> 8% of each run, Pallas kernels for 0% -> 0%
where the time goes in v1:
time: 899 us; the launch traced here: 892 us
  blocking collectives  454 us (51%)
  waiting for transfers between devices  274 us (30%)
  matrix products  55.9 us (6%)
  other arithmetic  36.5 us (4%)
  starting transfers between devices  31.8 us (4%)
  local copies, waits for them, and re-layouts  24.2 us (3%)
  between operations  15.8 us (2%)
    all_gather x1, blocking collectives, on_device(): lax.all_gather(norm_gain[0], 'dp', axis=0, tiled=True)  282 us
    unnamed x1, blocking collectives  172 us
    reduce_scatter x1, waiting for transfers between devices, on_device(): lax.psum_scatter(key_full_grad.astype(jnp.bfloat16), 'dp', scatter_dimens...  167 us
    ppermute x11, waiting for transfers between devices, passed_along(): return lax.ppermute(block, axis, route)  97.5 us
    ppermute x11, starting transfers between devices, passed_along(): return lax.ppermute(block, axis, route)  22.1 us
  transfers between devices with their start and end apart: 15, of which 7 were waited for; matrix products, arithmetic and copies ran while one was open for 8% of the time, Pallas kernels for 0%

profile of v1, /device:TPU:0, one launch (start us, length us, event | category | flops | bytes accessed | tf_op | source)
XLA Modules:
  0.0 892.4 jit_solution(11189655893695172834)
XLA Ops:
  7.2 0.7 exponential_bitcast_fusion.1
  8.1 1.7 fusion.72
  10.3 4.2 stack.31
  14.5 9.6 %all-to-all-start = ((bf16[32,256,512]{2,1,0:T(8,128)(2,1)}), bf16[32,256,512]{2,1,0:T(8,128)(2,1)}, u32[]{:S(2)}, u32[]{:S(2)}) async-start(bf16[32,256,512]{2,1,0:T(8,128)(2,1)} %stack.31), calls=%async_computation | async-start | bytes 16777216 | tf_op jit(solution)/shard_map/all_to_all | solution.py:92
  24.2 281.6 %all-gather = bf16[1,8192]{1,0:T(2,128)(2,1)S(1)} all-gather(bf16[1,256]{1,0:T(2,128)(2,1)S(1)} %copy-done.32), channel_id=2, replica_groups=mesh['pipe'=4,'dp'=32] {'dp'}, dimensions={1}, use_global_device_ids=true | all-gather | bytes 16896 | tf_op jit(solution)/shard_map/all_gather | solution.py:100
  306.4 0.7 copy.192
  307.3 2.1 fusion.2
  310.0 5.4 fusion.56
  315.7 9.4 %all-gather.3.cloned.1.call-done = bf16[8192,512]{1,0:T(8,128)(2,1)} async-done(((bf16[256,512]{1,0:T(8,128)(2,1)}), bf16[8192,512]{1,0:T(8,128)(2,1)}) %all-gather.3.cloned.1.call-update) | async-done | bytes 8388624 | tf_op jit(solution)/shard_map/all_gather | solution.py:90
  325.1 11.5 %copy.180 = bf16[512,8192]{1,0:T(8,128)(2,1)} copy(bf16[512,8192]{0,1:T(8,128)(2,1)} %bitcast.445) | data formatting | bytes 16777216 | tf_op jit(solution)/shard_map/dot_general | solution.py:110
  336.6 6.4 fusion.21
  343.1 1.3 collective-permute-start.3
  344.5 1.3 collective-permute-start.2
  345.8 1.3 collective-permute-start.1
  347.1 8.6 collective-permute-start
  355.7 0.7 fusion.102
  356.4 7.8 collective-permute-done
  364.2 0.7 fusion.105
  364.9 0.7 fusion.106
  365.6 0.7 fusion.104
  366.3 0.7 fusion.103
  367.0 3.3 fusion.32
  370.3 2.4 fusion.67
  376.2 1.0 fusion.18
  377.2 0.7 fusion.11
  377.9 0.6 fusion.59
  378.5 0.7 fusion.13
  379.2 0.6 fusion.60
  379.9 0.7 fusion.15
  380.6 0.6 fusion.61
  381.3 0.7 fusion.17
  382.0 0.6 fusion.62
  382.7 1.4 collective-permute-start.4
  384.2 1.3 collective-permute-start.5
  385.5 1.3 collective-permute-start.6
  386.8 1.5 collective-permute-start.7
  388.3 4.6 collective-permute-done.4
  392.9 9.4 %collective-permute-done.5 = bf16[2,128,4,128]{1,3,2,0:T(8,128)(2,1)S(1)} collective-permute-done((bf16[2,128,4,128]{1,3,2,0:T(8,128)(2,1)S(1)}, bf16[2,128,4,128]{1,3,2,0:T(8,128)(2,1)S(1)}, u32[]{:S(2)}, u32[]{:S(2)}) %collective-permute-start.5) | collective-permute-done | bytes 262176 | tf_op jit(solution)/shard_map/ppermute | solution.py:21
  403.5 5.7 convolution_convert_fusion
  409.3 2.4 fusion.20
  411.8 0.7 convert_add_fusion.4
  412.8 1.0 copy-done.2
  413.8 5.7 convolution_convert_fusion.1
  419.5 6.4 fusion.108
  425.9 6.0 multiply_reduce_fusion
  432.0 2.8 fusion.5
  434.8 1.3 collective-permute-start.8
  436.1 4.9 collective-permute-done.8
  441.0 4.9 fusion.6
  445.9 1.5 collective-permute-start.9
  447.4 70.7 %collective-permute-done.9 = bf16[128,8192]{1,0:T(8,128)(2,1)} collective-permute-done((bf16[128,8192]{1,0:T(8,128)(2,1)}, bf16[128,8192]{1,0:T(8,128)(2,1)}, u32[]{:S(2)}, u32[]{:S(2)}) %collective-permute-start.9) | collective-permute-done | bytes 2097184 | tf_op jit(solution)/shard_map/ppermute | solution.py:21
  518.2 6.0 fusion.7
  524.2 1.3 collective-permute-start.10
  525.4 1.2 dynamic-slice
  527.4 1.7 fusion.83
  529.6 0.8 copy-done.6
  531.8 0.8 copy-done.13
  532.6 0.7 multiply_convert_fusion
  533.4 1.3 copy.233
  534.7 172.4 %all-reduce = bf16[8192]{0:T(1024)(128)(2,1)S(1)} all-reduce(bf16[8192]{0:T(1024)(128)(2,1)S(1)} %get-tuple-element.25), channel_id=5, replica_groups=mesh['pipe'=4,'dp'=32] {'dp'}, use_global_device_ids=true, to_apply=%region_23.24.clone | all-reduce | flops 8192 | bytes 32768
  707.7 7.0 fusion.9
  714.7 1.8 bitcast_convert_fusion
  716.5 167.3 %reduce-scatter.3.cloned.1.call-done = bf16[256,512]{1,0:T(8,128)(2,1)} async-done(((bf16[8192,512]{1,0:T(8,128)(2,1)}), bf16[256,512]{1,0:T(8,128)(2,1)}) %reduce-scatter.3.cloned.1.call-update) | async-done | bytes 262160 | tf_op jit(solution)/shard_map/reduce_scatter | solution.py:256
  883.8 1.8 bitcast_convert_fusion.1
  (160 shorter events, 10.0 us)
Async XLA Ops:
  7.2 3.1 copy-start.25
  7.2 317.9 %all-gather.3.cloned.1.call-start = ((), (), s32[]{:S(2)}) async-start(), calls=%async_computation.3 | async-start | bytes 8650752 | tf_op jit(solution)/shard_map/all_gather | solution.py:90
  14.5 9.7 %copy-start.32 = (bf16[1,256]{1,0:T(2,128)(2,1)S(1)}, bf16[1,256]{1,0:T(2,128)(2,1)}, u32[]{:S(2)}) copy-start(bf16[1,256]{1,0:T(2,128)(2,1)} %param.13) | copy-start | bytes 1540
  14.5 291.4 %copy-start.37 = (s32[64]{0:T(128)S(1)}, s32[64]{0:T(128)}, u32[]{:S(2)}) copy-start(s32[64]{0:T(128)} %param.17) | copy-start | bytes 772
  14.5 291.7 %copy-start.10 = (bf16[1,128,4096]{2,1,0:T(8,128)(2,1)S(1)}, bf16[1,128,4096]{2,1,0:T(8,128)(2,1)}, u32[]{:S(2)}) copy-start(bf16[1,128,4096]{2,1,0:T(8,128)(2,1)} %param.10) | copy-start | bytes 3145732
  14.5 295.6 %all-to-all-start = ((bf16[32,256,512]{2,1,0:T(8,128)(2,1)}), bf16[32,256,512]{2,1,0:T(8,128)(2,1)}, u32[]{:S(2)}, u32[]{:S(2)}) async-start(bf16[32,256,512]{2,1,0:T(8,128)(2,1)} %stack.31), calls=%async_computation | async-start | bytes 16777216 | tf_op jit(solution)/shard_map/all_to_all | solution.py:92
  24.1 282.3 %copy-start.11 = (bf16[1,128,4096]{2,1,0:T(8,128)(2,1)S(1)}, bf16[1,128,4096]{2,1,0:T(8,128)(2,1)}, u32[]{:S(2)}) copy-start(bf16[1,128,4096]{2,1,0:T(8,128)(2,1)} %param.11) | copy-start | bytes 3145732
  24.1 690.6 %reduce-scatter.5.cloned.1.call-start = ((), (), s32[]{:S(2)}) async-start(), calls=%async_computation.5 | async-start | bytes 8650752 | tf_op jit(solution)/shard_map/reduce_scatter | solution.py:259
  305.8 30.8 %copy-start.26 = (f32[1,8192]{1,0:T(1,128)}, f32[1,8192]{1,0:T(1,128)S(1)}, u32[]{:S(2)}) copy-start(f32[1,8192]{1,0:T(1,128)S(1)} %convert_element_type.405) | copy-start | bytes 98308
  309.4 27.2 %copy-start.33 = (f32[128]{0:T(128)}, f32[128]{0:T(128)S(1)}, u32[]{:S(2)}) copy-start(f32[128]{0:T(128)S(1)} %add_sqrt_fusion) | copy-start | bytes 1540
  309.7 33.4 %copy-start.21 = (f32[128,64]{0,1:T(8,128)}, f32[128,64]{0,1:T(8,128)S(1)}, u32[]{:S(2)}) copy-start(f32[128,64]{0,1:T(8,128)S(1)} %get-tuple-element.56) | copy-start | bytes 98308
  309.7 33.4 %copy-start.23 = (f32[128,64]{0,1:T(8,128)}, f32[128,64]{0,1:T(8,128)S(1)}, u32[]{:S(2)}) copy-start(f32[128,64]{0,1:T(8,128)S(1)} %get-tuple-element.57) | copy-start | bytes 98308
  315.7 58.7 %copy-start.20 = (bf16[128,4,128,1]{0,2,3,1:T(8,128)(2,1)}, bf16[128,4,128,1]{0,2,3,1:T(8,128)(2,1)S(1)}, u32[]{:S(2)}) copy-start(bf16[128,4,128,1]{0,2,3,1:T(8,128)(2,1)S(1)} %copy.249) | copy-start | bytes 393220
  343.1 23.1 %collective-permute-start.3 = (bf16[2,128,4,128]{1,3,2,0:T(8,128)(2,1)S(1)}, bf16[2,128,4,128]{1,3,2,0:T(8,128)(2,1)S(1)}, u32[]{:S(2)}, u32[]{:S(2)}) collective-permute-start(bf16[2,128,4,128]{1,3,2,0:T(8,128)(2,1)S(1)} %pad_maximum_fusion), channel_id=1, source_target_pairs={{0,1},{1,2},{2,3},{3,4},{4,5},{5,6},{6,7},{7,8},{8,9},{9,10},{10,1... | collective-permute-start | bytes 786440 | tf_op jit(solution)/shard_map/ppermute | solution.py:21
  344.5 21.1 %collective-permute-start.2 = (bf16[2,128,4,128]{1,3,2,0:T(8,128)(2,1)S(1)}, bf16[2,128,4,128]{1,3,2,0:T(8,128)(2,1)S(1)}, u32[]{:S(2)}, u32[]{:S(2)}) collective-permute-start(bf16[2,128,4,128]{1,3,2,0:T(8,128)(2,1)S(1)} %pad_maximum_fusion), channel_id=1, source_target_pairs={{0,2},{1,3},{2,4},{3,5},{4,6},{5,7},{6,8},{7,9},{8,10},{9,11},{10,... | collective-permute-start | bytes 786440 | tf_op jit(solution)/shard_map/ppermute | solution.py:21
  345.8 19.1 %collective-permute-start.1 = (bf16[2,128,4,128]{1,3,2,0:T(8,128)(2,1)S(1)}, bf16[2,128,4,128]{1,3,2,0:T(8,128)(2,1)S(1)}, u32[]{:S(2)}, u32[]{:S(2)}) collective-permute-start(bf16[2,128,4,128]{1,3,2,0:T(8,128)(2,1)S(1)} %pad_maximum_fusion), channel_id=1, source_target_pairs={{0,3},{1,4},{2,5},{3,6},{4,7},{5,8},{6,9},{7,10},{8,11},{9,12},{10... | collective-permute-start | bytes 786440 | tf_op jit(solution)/shard_map/ppermute | solution.py:21
  347.1 17.1 %collective-permute-start = (bf16[2,128,4,128]{1,3,2,0:T(8,128)(2,1)S(1)}, bf16[2,128,4,128]{1,3,2,0:T(8,128)(2,1)S(1)}, u32[]{:S(2)}, u32[]{:S(2)}) collective-permute-start(bf16[2,128,4,128]{1,3,2,0:T(8,128)(2,1)S(1)} %pad_maximum_fusion), channel_id=1, source_target_pairs={{0,4},{1,5},{2,6},{3,7},{4,8},{5,9},{6,10},{7,11},{8,12},{9,13},{1... | collective-permute-start | bytes 786440 | tf_op jit(solution)/shard_map/ppermute | solution.py:21
  356.4 13.9 %copy-start = (f32[4,8,128,128]{2,3,1,0:T(8,128)}, f32[4,8,128,128]{2,3,1,0:T(8,128)S(1)}, u32[]{:S(2)}) copy-start(f32[4,8,128,128]{2,3,1,0:T(8,128)S(1)} %get-tuple-element.59) | copy-start | bytes 6291460
  364.2 13.0 %copy-start.16 = (bf16[2,128,4,128]{1,3,2,0:T(8,128)(2,1)}, bf16[2,128,4,128]{1,3,2,0:T(8,128)(2,1)S(1)}, u32[]{:S(2)}) copy-start(bf16[2,128,4,128]{1,3,2,0:T(8,128)(2,1)S(1)} %collective-permute-done) | copy-start | bytes 786436
  364.9 13.6 %copy-start.14 = (bf16[2,128,4,128]{1,3,2,0:T(8,128)(2,1)}, bf16[2,128,4,128]{1,3,2,0:T(8,128)(2,1)S(1)}, u32[]{:S(2)}) copy-start(bf16[2,128,4,128]{1,3,2,0:T(8,128)(2,1)S(1)} %collective-permute-done.1) | copy-start | bytes 786436
  366.3 15.0 %copy-start.18 = (bf16[2,128,4,128]{1,3,2,0:T(8,128)(2,1)}, bf16[2,128,4,128]{1,3,2,0:T(8,128)(2,1)S(1)}, u32[]{:S(2)}) copy-start(bf16[2,128,4,128]{1,3,2,0:T(8,128)(2,1)S(1)} %collective-permute-done.3) | copy-start | bytes 786436
  370.3 10.9 %copy-start.30 = (f32[4,8,128]{2,1,0:T(8,128)}, f32[4,8,128]{2,1,0:T(8,128)S(1)}, u32[]{:S(2)}) copy-start(f32[4,8,128]{2,1,0:T(8,128)S(1)} %add_add_fusion) | copy-start | bytes 49156
  377.2 4.1 copy-start.31
  379.2 1.4 copy-start.5
  380.6 1.4 copy-start.7
  382.0 4.9 copy-start.12
  382.7 20.8 %copy-start.1 = (bf16[1,128,8192]{2,1,0:T(8,128)(2,1)S(1)}, bf16[1,128,8192]{2,1,0:T(8,128)(2,1)}, u32[]{:S(2)}) copy-start(bf16[1,128,8192]{2,1,0:T(8,128)(2,1)} %param.9) | copy-start | bytes 6291460
  382.7 20.8 %copy-start.27 = (f32[1,8192]{1,0:T(1,128)S(1)}, f32[1,8192]{1,0:T(1,128)}, u32[]{:S(2)}) copy-start(f32[1,8192]{1,0:T(1,128)} %copy-done.26) | copy-start | bytes 98308
  382.7 20.8 %copy-start.34 = (f32[128]{0:T(128)S(1)}, f32[128]{0:T(128)}, u32[]{:S(2)}) copy-start(f32[128]{0:T(128)} %copy-done.33) | copy-start | bytes 1540
  382.7 10.2 %collective-permute-start.4 = (bf16[2,128,4,128]{1,3,2,0:T(8,128)(2,1)S(1)}, bf16[2,128,4,128]{1,3,2,0:T(8,128)(2,1)S(1)}, u32[]{:S(2)}, u32[]{:S(2)}) collective-permute-start(bf16[2,128,4,128]{1,3,2,0:T(8,128)(2,1)S(1)} %pad_maximum_fusion.1), channel_id=1, source_target_pairs={{1,0},{2,1},{3,2},{4,3},{5,4},{6,5},{7,6},{8,7},{9,8},{10,9},{11,1... | collective-permute-start | bytes 786440 | tf_op jit(solution)/shard_map/ppermute | solution.py:21
  384.2 18.2 %collective-permute-start.5 = (bf16[2,128,4,128]{1,3,2,0:T(8,128)(2,1)S(1)}, bf16[2,128,4,128]{1,3,2,0:T(8,128)(2,1)S(1)}, u32[]{:S(2)}, u32[]{:S(2)}) collective-permute-start(bf16[2,128,4,128]{1,3,2,0:T(8,128)(2,1)S(1)} %pad_maximum_fusion.2), channel_id=1, source_target_pairs={{2,0},{3,1},{4,2},{5,3},{6,4},{7,5},{8,6},{9,7},{10,8},{11,9},{12,... | collective-permute-start | bytes 786440 | tf_op jit(solution)/shard_map/ppermute | solution.py:21
  385.5 16.9 %collective-permute-start.6 = (bf16[2,128,4,128]{1,3,2,0:T(8,128)(2,1)S(1)}, bf16[2,128,4,128]{1,3,2,0:T(8,128)(2,1)S(1)}, u32[]{:S(2)}, u32[]{:S(2)}) collective-permute-start(bf16[2,128,4,128]{1,3,2,0:T(8,128)(2,1)S(1)} %pad_maximum_fusion.3), channel_id=1, source_target_pairs={{3,0},{4,1},{5,2},{6,3},{7,4},{8,5},{9,6},{10,7},{11,8},{12,9},{13... | collective-permute-start | bytes 786440 | tf_op jit(solution)/shard_map/ppermute | solution.py:21
  386.8 15.5 %collective-permute-start.7 = (bf16[2,128,4,128]{1,3,2,0:T(8,128)(2,1)S(1)}, bf16[2,128,4,128]{1,3,2,0:T(8,128)(2,1)S(1)}, u32[]{:S(2)}, u32[]{:S(2)}) collective-permute-start(bf16[2,128,4,128]{1,3,2,0:T(8,128)(2,1)S(1)} %pad_maximum_fusion.4), channel_id=1, source_target_pairs={{4,0},{5,1},{6,2},{7,3},{8,4},{9,5},{10,6},{11,7},{12,8},{13,9},{1... | collective-permute-start | bytes 786440 | tf_op jit(solution)/shard_map/ppermute | solution.py:21
  392.9 9.9 %copy-start.38 = (bf16[2,128,4,128]{1,3,2,0:T(8,128)(2,1)}, bf16[2,128,4,128]{1,3,2,0:T(8,128)(2,1)S(1)}, u32[]{:S(2)}) copy-start(bf16[2,128,4,128]{1,3,2,0:T(8,128)(2,1)S(1)} %collective-permute-done.4) | copy-start | bytes 786436
  402.4 0.7 copy-start.40
  402.4 0.8 copy-start.42
  402.4 0.9 copy-start.44
  402.9 0.6 copy-start.46
  409.2 474.6 %reduce-scatter.3.cloned.1.call-start = ((), (), s32[]{:S(2)}) async-start(), calls=%async_computation.4 | async-start | bytes 8650752 | tf_op jit(solution)/shard_map/reduce_scatter | solution.py:256
  409.3 2.5 copy-start.39
  409.3 2.5 copy-start.41
  409.3 2.5 copy-start.43
  409.3 2.5 copy-start.45
  411.8 1.0 copy-start.9
  411.8 1.0 copy-start.22
  411.8 1.0 copy-start.24
  411.8 2.0 copy-start.2
  411.8 2.0 copy-start.28
  411.8 2.0 copy-start.35
  419.5 6.4 copy-start.3
  419.5 6.4 copy-start.47
  425.9 6.1 copy-start.4
  425.9 6.1 copy-start.29
  425.9 6.1 copy-start.36
  434.8 6.2 collective-permute-start.8
  445.9 72.2 %collective-permute-start.9 = (bf16[128,8192]{1,0:T(8,128)(2,1)}, bf16[128,8192]{1,0:T(8,128)(2,1)}, u32[]{:S(2)}, u32[]{:S(2)}) collective-permute-start(bf16[128,8192]{1,0:T(8,128)(2,1)} %fusion.6), channel_id=1, source_target_pairs={{32,0},{64,32},{96,64},{33,1},{65,33},{97,65},{34,2},{66,34},{98,6... | collective-permute-start | bytes 6291464 | tf_op jit(solution)/shard_map/ppermute | solution.py:21
  524.2 183.5 %collective-permute-start.10 = (bf16[128,8192]{1,0:T(8,128)(2,1)}, bf16[128,8192]{1,0:T(8,128)(2,1)}, u32[]{:S(2)}, u32[]{:S(2)}) collective-permute-start(bf16[128,8192]{1,0:T(8,128)(2,1)} %fusion.7), channel_id=1, source_target_pairs={{32,0},{64,32},{96,64},{33,1},{65,33},{97,65},{34,2},{66,34},{98,6... | collective-permute-start | bytes 6291464 | tf_op jit(solution)/shard_map/ppermute | solution.py:21
  527.3 1.8 copy-start.8
  529.1 1.2 copy-start.6
  529.1 1.3 copy-start.15
  530.4 1.0 copy-start.17
  531.3 1.2 copy-start.13
  531.3 1.3 copy-start.19
Sparse Core Ops, SparseCore 0:
  10.2 314.8 all-gather.2
  409.3 213.8 reduce-scatter.4
  625.7 258.0 reduce-scatter.2
